TPU v7x, 32 devices: a whole 2x2x4 slice. The times are simulated.
32 devices in a mesh: grp: 2 (over y), gene: 4 (over z), row: 4 (over x, core).
Axes of the slice: x: 2, y: 2, z: 4, core: 2. Of those that a mesh axis runs over, the one named last changes fastest.
Arguments:
- x_slab: bfloat16 [24576, 2560], P(('grp', 'row'), 'gene'), parts along dimension 0, may hold values from -6 to 6
- cell_factor: bfloat16 [4096, 128], P(('grp', 'row')), parts along dimension 0, may hold values from -1.5 to 1.5
- row_index: int32 [24576], P(('grp', 'row')), parts along dimension 0, may hold values from 0 to 2047, as said below
- gene_scale: float32 [5120], P(('grp', 'gene')), parts along dimension 0, may hold values from 0.3 to 3
- gene_factor: float32 [5120, 128], P(('grp', 'gene', 'row')), parts along dimension 0, may hold values from -1.5 to 1.5
- first_moment: float32 [5120, 128], P(('grp', 'gene', 'row')), parts along dimension 0, may hold values from -1.2 to 1.2
- second_moment: float32 [5120, 128], P(('grp', 'gene', 'row')), parts along dimension 0, may hold values from 0.05 to 1
Outputs:
- grad_cells: float32 [24576, 128], P(('grp', 'row', 'gene')), parts along dimension 0
- new_factor: float32 [5120, 128], P(('grp', 'gene', 'row')), parts along dimension 0
- new_first: float32 [5120, 128], P(('grp', 'gene', 'row')), parts along dimension 0
- new_second: float32 [5120, 128], P(('grp', 'gene', 'row')), parts along dimension 0
There are 2 independent parts, one for each index of `grp`. A program takes and returns all parts, laid end to end along the dimension named above; each array names one. Nothing has to cross between parts.
Inputs may be any that keep to these rules, and one draw needn't show every extreme that they name: `row_index`: rows r * 3072 to (r + 1) * 3072 - 1 name cells r * 512 to (r + 1) * 512 - 1; cells may repeat.
All inputs are finite; a program needn't handle non-finite values.
Results may differ from a plain program's by a relative error of at most 0.008.
Values may be sent and summed in bfloat16 or wider, within the bound.
A program may use at most 64 MiB of HBM per device.

v0:
```python
import math

import jax
import jax.numpy as jnp
from jax import lax
from jax.sharding import PartitionSpec as P

tukey_c = 4.685
beta_one = 0.9
beta_two = 0.999
learn_rate = 0.02
adam_eps = 1e-08


def influence(factors, x_slab, gene_scale, piece):
    pred = lax.dot_general(
        factors, piece, (((1,), (1,)), ((), ())), preferred_element_type=jnp.float32
    )
    x_part = x_slab.astype(jnp.float32)
    scaled = (x_part - pred) / gene_scale[None, :]
    ratio = scaled / tukey_c
    inside = 1.0 - ratio * ratio
    weight = jnp.where(jnp.abs(ratio) < 1.0, inside * inside, 0.0)
    return (scaled * weight / gene_scale[None, :]).astype(jnp.bfloat16)


def local(x_slab, cell_factor, row_index, gene_scale, gene_factor, first_moment, second_moment):
    rows_dev, genes_dev = x_slab.shape
    cells_dev = cell_factor.shape[0]
    n_gene = lax.axis_size("gene")
    local_index = row_index - lax.axis_index("row") * cells_dev
    factors = jnp.take(cell_factor, local_index, axis=0)
    factor_bf = gene_factor.astype(jnp.bfloat16)
    scale_k = 4.0 / math.sqrt(genes_dev * n_gene)
    gathered = lax.all_gather(factor_bf, "row", axis=0, tiled=True)
    infl = influence(factors, x_slab, gene_scale, gathered)
    grad_rows = jnp.dot(infl, gathered, preferred_element_type=jnp.float32)
    grad_cols = lax.dot_general(
        infl, factors, (((0,), (0,)), ((), ())), preferred_element_type=jnp.float32
    )
    grad_genes = lax.psum_scatter(
        (-scale_k * grad_cols).astype(jnp.bfloat16), "row", scatter_dimension=0, tiled=True
    ).astype(jnp.float32)
    grad_cells = lax.psum_scatter(-scale_k * grad_rows, "gene", scatter_dimension=0, tiled=True)
    new_first = beta_one * first_moment + (1.0 - beta_one) * grad_genes
    new_second = beta_two * second_moment + (1.0 - beta_two) * grad_genes * grad_genes
    first_hat = new_first / (1.0 - beta_one**10)
    second_hat = new_second / (1.0 - beta_two**10)
    new_factor = gene_factor - learn_rate * first_hat / (jnp.sqrt(second_hat) + adam_eps)
    return (grad_cells, new_factor, new_first, new_second)


def solution(mesh):
    in_specs = (
        P(("grp", "row"), "gene"),
        P(("grp", "row"), None),
        P(("grp", "row")),
        P(("grp", "gene")),
        P(("grp", "gene", "row"), None),
        P(("grp", "gene", "row"), None),
        P(("grp", "gene", "row"), None),
    )
    out_specs = (
        P(("grp", "row", "gene"), None),
        P(("grp", "gene", "row"), None),
        P(("grp", "gene", "row"), None),
        P(("grp", "gene", "row"), None),
    )
    return jax.shard_map(local, mesh=mesh, in_specs=in_specs, out_specs=out_specs, check_vma=False)
```

profile of v0, /device:TPU:0, one launch (start us, length us, event | category | flops | bytes accessed | tf_op | source)
XLA Modules:
  0.0 102.3 jit_solution(13833262780194311443)
XLA Ops:
  7.2 0.0 copy-start
  7.2 0.0 copy-start.5
  7.2 0.0 reduce-scatter.5.cloned.1.call-start
  7.2 0.7 compare_and_fusion
  8.0 0.7 fusion.3
  8.7 0.9 convert_element_type.16
  9.6 6.7 %all_gather.3 = bf16[640,128]{1,0:T(8,128)(2,1)S(1)} all-gather(bf16[160,128]{1,0:T(8,128)(2,1)S(1)} %convert_element_type.16), channel_id=1, replica_groups=mesh['grp'=2,'gene'=4,'row'=4] {'row'}, dimensions={0}, use_global_device_ids=true | all-gather | bytes 204800 | tf_op jit(solution)/shard_map/all_gather | solution.py:35
  16.2 0.0 copy-done
  16.2 9.2 %gather_fusion = bf16[3072,128]{1,0:T(8,128)(2,1)S(1)} fusion(bf16[512,128]{1,0:T(8,128)(2,1)S(1)} %copy-done, s32[3072]{0:T(1024)S(1)} %fusion.3), kind=kCustom, calls=%fused_computation | custom fusion | bytes 1585152 | tf_op jit(solution)/shard_map/jit(_take)/gather | solution.py:32
  25.4 0.0 copy-done.5
  25.4 6.0 %divide_convert_fusion = bf16[3072,640]{1,0:T(8,128)(2,1)S(1)} fusion(bf16[3072,640]{1,0:T(8,128)(2,1)} %param.7, bf16[640,128]{1,0:T(8,128)(2,1)S(1)} %all_gather.3, f32[640]{0:T(1024)S(1)} %copy-done.5, bf16[3072,128]{1,0:T(8,128)(2,1)S(1)} %gather_fusion, pred[3072]{0:T(1024)(128)(4,1)S(1)} %compare_and_fusion), kind=kOutput, calls=%fused_computation.1 | convolution fusion | flops 529268736 | bytes 8820224 | tf_op jit(solution)/shard_map/dot_general | solution.py:16
  31.4 0.0 copy-start.1
  31.4 1.9 %copy-done.1 = bf16[3072,640]{1,0:T(8,128)(2,1)} copy-done((bf16[3072,640]{1,0:T(8,128)(2,1)}, bf16[3072,640]{1,0:T(8,128)(2,1)S(1)}, u32[]{:S(2)}) %copy-start.1) | copy-done | bytes 3932184
  33.2 2.4 %fusion = bf16[640,128]{1,0:T(8,128)(2,1)} fusion(bf16[3072,640]{1,0:T(8,128)(2,1)S(1)} %divide_convert_fusion, bf16[3072,128]{1,0:T(8,128)(2,1)S(1)} %gather_fusion, pred[3072]{0:T(1024)(128)(4,1)S(1)} %compare_and_fusion), kind=kOutput, calls=%fused_computation.5 | convolution fusion | flops 503873536 | bytes 4885504 | tf_op jit(solution)/shard_map/dot_general | solution.py:38
  35.7 0.0 reduce-scatter.5.cloned.1.call-update
  35.7 0.0 copy-start.2
  35.7 0.0 copy-start.3
  35.7 0.0 copy-start.4
  35.7 0.0 reduce-scatter.3.cloned.1.call-start
  35.8 4.5 %convolution_multiply_fusion = f32[3072,128]{1,0:T(8,128)} fusion(bf16[3072,640]{1,0:T(8,128)(2,1)} %copy-done.1, bf16[640,128]{1,0:T(8,128)(2,1)S(1)} %all_gather.3), kind=kOutput, calls=%fused_computation.3 | convolution fusion | flops 503709696 | bytes 5668864 | tf_op jit(solution)/shard_map/dot_general | solution.py:37
  40.3 0.0 reduce-scatter.3.cloned.1.call-update
  40.3 16.8 %reduce-scatter.5.cloned.1.call-done = bf16[160,128]{1,0:T(8,128)(2,1)} async-done(((bf16[640,128]{1,0:T(8,128)(2,1)}), bf16[160,128]{1,0:T(8,128)(2,1)}) %reduce-scatter.5.cloned.1.call-update) | async-done | bytes 40976 | tf_op jit(solution)/shard_map/reduce_scatter | solution.py:41
  57.1 0.0 copy-done.2
  57.1 0.0 copy-done.3
  57.1 0.0 copy-done.4
  57.1 1.5 %divide_subtract_fusion = (f32[160,128]{1,0:T(8,128)}, f32[160,128]{1,0:T(8,128)}, f32[160,128]{1,0:T(8,128)}) fusion(f32[160,128]{1,0:T(8,128)S(1)} %copy-done.2, bf16[160,128]{1,0:T(8,128)(2,1)} %reduce-scatter.5.cloned.1.call-done, f32[160,128]{1,0:T(8,128)S(1)} %copy-done.3, f32[160,128]{1,0:T(8,128)S(1)} %copy-done.4), kind=kLoop, calls=%fused_computation.11 | loop fusion | flops 266240 | bytes 532480 | tf_op jit(solution)/shard_map/sub | solution.py:49
  58.6 36.8 %reduce-scatter.3.cloned.1.call-done = f32[768,128]{1,0:T(8,128)} async-done(((f32[3072,128]{1,0:T(8,128)}), f32[768,128]{1,0:T(8,128)}) %reduce-scatter.3.cloned.1.call-update) | async-done | bytes 393232 | tf_op jit(solution)/shard_map/reduce_scatter | solution.py:44
Async XLA Ops:
  7.2 9.1 %copy-start = (bf16[512,128]{1,0:T(8,128)(2,1)S(1)}, bf16[512,128]{1,0:T(8,128)(2,1)}, u32[]{:S(2)}) copy-start(bf16[512,128]{1,0:T(8,128)(2,1)} %param.8) | copy-start | bytes 393220
  7.2 18.2 %copy-start.5 = (f32[640]{0:T(1024)S(1)}, f32[640]{0:T(1024)}, u32[]{:S(2)}) copy-start(f32[640]{0:T(1024)} %param.10) | copy-start | bytes 7684
  7.2 49.9 %reduce-scatter.5.cloned.1.call-start = ((), (), s32[]{:S(2)}) async-start(), calls=%async_computation.3 | async-start | bytes 204800 | tf_op jit(solution)/shard_map/reduce_scatter | solution.py:41
  31.4 1.9 %copy-start.1 = (bf16[3072,640]{1,0:T(8,128)(2,1)}, bf16[3072,640]{1,0:T(8,128)(2,1)S(1)}, u32[]{:S(2)}) copy-start(bf16[3072,640]{1,0:T(8,128)(2,1)S(1)} %divide_convert_fusion) | copy-start | bytes 11796484
  35.7 21.4 %copy-start.2 = (f32[160,128]{1,0:T(8,128)S(1)}, f32[160,128]{1,0:T(8,128)}, u32[]{:S(2)}) copy-start(f32[160,128]{1,0:T(8,128)} %param.11) | copy-start | bytes 245764
  35.7 21.4 %copy-start.3 = (f32[160,128]{1,0:T(8,128)S(1)}, f32[160,128]{1,0:T(8,128)}, u32[]{:S(2)}) copy-start(f32[160,128]{1,0:T(8,128)} %param.12) | copy-start | bytes 245764
  35.7 21.4 %copy-start.4 = (f32[160,128]{1,0:T(8,128)S(1)}, f32[160,128]{1,0:T(8,128)}, u32[]{:S(2)}) copy-start(f32[160,128]{1,0:T(8,128)} %param.13) | copy-start | bytes 245764
  35.7 59.7 %reduce-scatter.3.cloned.1.call-start = ((), (), s32[]{:S(2)}) async-start(), calls=%async_computation.2 | async-start | bytes 1966080 | tf_op jit(solution)/shard_map/reduce_scatter | solution.py:44
Sparse Core Ops, SparseCore 0:
  35.8 21.2 reduce-scatter.4
  60.0 35.4 reduce-scatter.2
where the time goes:
time: 103 us; the launch traced here: 102 us
  waiting for transfers between devices  53.7 us (52%)
  between operations  14.1 us (14%)
  matrix products  12.9 us (13%)
  local copies, waits for them, and re-layouts  11 us (11%)
  blocking collectives  6.67 us (6%)
  other arithmetic  3.82 us (4%)
    reduce_scatter x1, waiting for transfers between devices, local(): lax.psum_scatter(-scale_k * grad_rows, 'gene', scatter_dimension=0, tiled...  36.8 us
    reduce_scatter x1, waiting for transfers between devices, local(): lax.psum_scatter((-scale_k * grad_cols).astype(jnp.bfloat16), 'row', scat...  16.8 us
    gather x1, local copies, waits for them, and re-layouts, local(): factors = jnp.take(cell_factor, local_index, axis=0)  9.15 us
    all_gather x1, blocking collectives, local(): gathered = lax.all_gather(factor_bf, 'row', axis=0, tiled=True)  6.67 us
    dot_general x1, matrix products, influence(): lax.dot_general(factors, piece, (((1,), (1,)), ((), ())), preferred_eleme...  5.96 us
    dot_general x1, matrix products, local(): grad_rows = jnp.dot(infl, gathered, preferred_element_type=jnp.float32)  4.49 us
    dot_general x1, matrix products, local(): lax.dot_general(infl, factors, (((0,), (0,)), ((), ())), preferred_elemen...  2.42 us
  transfers between devices with their start and end apart: 2, of which 2 were waited for; matrix products, arithmetic and copies ran while one was open for 6% of the time, Pallas kernels for 0%

commit v1 on v0

v1 whole, which is shorter than its diff:
```python
import functools
import math

import jax
import jax.numpy as jnp
from jax import lax
from jax.experimental import pallas as pl
from jax.experimental.pallas import tpu as pltpu
from jax.sharding import PartitionSpec as P

tukey_c = 4.685
beta_one = 0.9
beta_two = 0.999
learn_rate = 0.02
adam_eps = 1e-08
MESH = pl.DeviceIdType.MESH
LANES = 128


def plan(rows, n_gene):
    per = rows // n_gene
    if per >= 256:
        chunk = 256 if per % 256 == 0 else per
        return per, chunk, per // chunk, 1
    group = max(g for g in range(1, n_gene + 1) if n_gene % g == 0 and g * per <= 384 and (g * per) % LANES == 0)
    return per, per * group, 1, group


def kernel(
    n_gene,
    n_row,
    x_hbm,
    cell_ref,
    index_ref,
    scale_ref,
    gene_ref,
    rows_out,
    genes_out,
    x_buf,
    fac,
    fac_t,
    gath,
    gath_t,
    cols,
    send_buf,
    recv_buf,
    own,
    col_send,
    col_recv,
    x_sem,
    ag_send_sem,
    ag_recv_sem,
    send_sem,
    recv_sem,
    col_send_sem,
    col_recv_sem,
):
    rows, genes = x_buf.shape
    cells, rank = cell_ref.shape
    genes_own = gene_ref.shape[0]
    per, chunk, pieces, group = plan(rows, n_gene)
    n_chunk = rows // chunk
    own_chunks = pieces
    me_gene = lax.axis_index("gene")
    me_row = lax.axis_index("row")

    barrier = pltpu.get_barrier_semaphore()
    for step in range(1, n_row):
        pl.semaphore_signal(barrier, inc=1, device_id={"row": lax.rem(me_row + step, n_row)}, device_id_type=MESH)
    for step in range(1, n_gene):
        pl.semaphore_signal(barrier, inc=1, device_id={"gene": lax.rem(me_gene + step, n_gene)}, device_id_type=MESH)

    if group == 1:
        first = me_gene * pieces + pieces
    else:
        first = me_gene // group + 1

    def chunk_at(i):
        return lax.rem(first + i, n_chunk)

    def x_copy(i):
        window = pl.ds(pl.multiple_of(chunk_at(i) * chunk, chunk), chunk)
        return pltpu.make_async_copy(x_hbm.at[window], x_buf.at[pl.ds(i * chunk, chunk)], x_sem.at[i])

    for i in range(n_chunk):
        x_copy(i).start()

    own_genes = pl.ds(pl.multiple_of(me_row * genes_own, genes_own), genes_own)
    gath[own_genes] = gene_ref[...].astype(jnp.bfloat16)

    cell_t = cell_ref[...].astype(jnp.float32).T.astype(jnp.bfloat16)
    cell_id = lax.broadcasted_iota(jnp.int32, (cells, LANES), 0) + me_row * cells

    def gather_factors(c):
        parts = []
        for k in range(chunk // LANES):
            at = c * (chunk // LANES) + k
            hit = (cell_id == index_ref[pl.ds(at, 1), :]).astype(jnp.float32).astype(jnp.bfloat16)
            parts.append(jnp.dot(cell_t, hit, preferred_element_type=jnp.float32))
        both = jnp.concatenate(parts, axis=1)
        fac_t[c] = both.astype(jnp.bfloat16)
        fac[c] = both.T.astype(jnp.bfloat16)

    half = n_chunk // 2
    for c in range(half):
        gather_factors(c)

    pl.semaphore_wait(barrier, n_row + n_gene - 2)

    def ag_copy(step):
        peer = lax.rem(me_row + step, n_row)
        return pltpu.make_async_remote_copy(
            src_ref=gath.at[own_genes],
            dst_ref=gath.at[own_genes],
            send_sem=ag_send_sem.at[step - 1],
            recv_sem=ag_recv_sem.at[step - 1],
            device_id={"row": peer},
            device_id_type=MESH,
        )

    for step in range(1, n_row):
        ag_copy(step).start()
    for c in range(half, n_chunk):
        gather_factors(c)
    inv = 1.0 / scale_ref[...]
    inv_tc = inv * (1.0 / tukey_c)
    inv_sq = inv * inv
    for step in range(1, n_row):
        ag_copy(step).wait()
    factor = gath[...]
    gath_t[...] = factor.astype(jnp.float32).T.astype(jnp.bfloat16)

    def block_copy(i, j):
        c = chunk_at(i)
        owner = c // pieces if group == 1 else c * group + j
        piece = lax.rem(c, pieces) if group == 1 else 0
        size = chunk if group == 1 else per
        return pltpu.make_async_remote_copy(
            src_ref=send_buf.at[i, pl.ds(j * size, size)],
            dst_ref=recv_buf.at[me_gene, piece],
            send_sem=send_sem.at[i, j],
            recv_sem=recv_sem.at[me_gene, piece],
            device_id={"gene": owner},
            device_id_type=MESH,
        )

    for i in range(n_chunk):
        c = chunk_at(i)
        x_copy(i).wait()
        f = fac[c]
        pred = jnp.dot(f, gath_t[...], preferred_element_type=jnp.float32)
        resid = x_buf[i * chunk : (i + 1) * chunk].astype(jnp.float32) - pred
        ratio = resid * inv_tc
        inside = jnp.maximum(1.0 - ratio * ratio, 0.0)
        infl = (resid * inv_sq * (inside * inside)).astype(jnp.bfloat16)
        part = jnp.dot(infl, gath[...], preferred_element_type=jnp.float32)
        if group == 1 and i >= n_chunk - own_chunks:
            own[i - (n_chunk - own_chunks)] = part
        else:
            send_buf[i] = part.astype(jnp.bfloat16)
            if group > 1:
                for j in range(group):

                    @pl.when(c * group + j == me_gene)
                    def _():
                        own[0] = part[j * per : (j + 1) * per]

        add = jnp.dot(fac_t[c], infl, preferred_element_type=jnp.float32)
        cols[...] = add if i == 0 else cols[...] + add
        if group == 1:
            if i < n_chunk - own_chunks:
                block_copy(i, 0).start()
        else:
            for j in range(group):

                @pl.when(c * group + j != me_gene)
                def _():
                    block_copy(i, j).start()

    total = cols[...].T
    col_send[...] = total.astype(jnp.bfloat16)
    cols_own = jnp.zeros((genes_own, rank), jnp.float32)

    def col_copy(step):
        peer = lax.rem(me_row + step, n_row)
        return pltpu.make_async_remote_copy(
            src_ref=col_send.at[pl.ds(pl.multiple_of(peer * genes_own, genes_own), genes_own)],
            dst_ref=col_recv.at[step - 1],
            send_sem=col_send_sem.at[step - 1],
            recv_sem=col_recv_sem.at[step - 1],
            device_id={"row": peer},
            device_id_type=MESH,
        )

    for step in range(1, n_row):
        col_copy(step).start()
    cols_own = col_send[own_genes].astype(jnp.float32)
    for step in range(1, n_row):
        col_copy(step).wait()
        cols_own = cols_own + col_recv[step - 1].astype(jnp.float32)
    genes_out[...] = cols_own

    size = chunk if group == 1 else per

    def arrived(step, piece):
        sender = lax.rem(me_gene + n_gene - step, n_gene)
        copy = pltpu.make_async_remote_copy(
            src_ref=recv_buf.at[sender, piece],
            dst_ref=recv_buf.at[sender, piece],
            send_sem=send_sem.at[0, 0],
            recv_sem=recv_sem.at[sender, piece],
            device_id={"gene": sender},
            device_id_type=MESH,
        )
        copy.wait_recv()
        return recv_buf[sender, piece].astype(jnp.float32)

    for piece in range(pieces):
        acc = own[piece]
        for step in range(1, n_gene):
            acc = acc + arrived(step, piece)
        rows_out[piece * size : (piece + 1) * size] = acc

    for i in range(n_chunk):
        if group == 1:
            if i < n_chunk - own_chunks:
                block_copy(i, 0).wait_send()
        else:
            for j in range(group):

                @pl.when(chunk_at(i) * group + j != me_gene)
                def _():
                    block_copy(i, j).wait_send()


def fused(n_gene, n_row, x_slab, cell_factor, index, scale, gene_factor):
    rows, genes = x_slab.shape
    cells, rank = cell_factor.shape
    genes_own = gene_factor.shape[0]
    per, chunk, pieces, group = plan(rows, n_gene)
    n_chunk = rows // chunk
    size = chunk if group == 1 else per
    vmem = pl.BlockSpec(memory_space=pltpu.VMEM)
    bf = jnp.bfloat16
    dma = pltpu.SemaphoreType.DMA
    return pl.pallas_call(
        functools.partial(kernel, n_gene, n_row),
        out_shape=(
            jax.ShapeDtypeStruct((per, rank), jnp.float32),
            jax.ShapeDtypeStruct((genes_own, rank), jnp.float32),
        ),
        in_specs=[pl.BlockSpec(memory_space=pl.ANY), vmem, vmem, vmem, vmem],
        out_specs=(vmem, vmem),
        scratch_shapes=[
            pltpu.VMEM((rows, genes), bf),
            pltpu.VMEM((n_chunk, chunk, rank), bf),
            pltpu.VMEM((n_chunk, rank, chunk), bf),
            pltpu.VMEM((genes, rank), bf),
            pltpu.VMEM((rank, genes), bf),
            pltpu.VMEM((rank, genes), jnp.float32),
            pltpu.VMEM((n_chunk, chunk, rank), bf),
            pltpu.VMEM((n_gene, pieces, size, rank), bf),
            pltpu.VMEM((pieces, size, rank), jnp.float32),
            pltpu.VMEM((genes, rank), bf),
            pltpu.VMEM((n_row - 1, genes_own, rank), bf),
            dma((n_chunk,)),
            dma((n_row - 1,)),
            dma((n_row - 1,)),
            dma((n_chunk, group)),
            dma((n_gene, pieces)),
            dma((n_row - 1,)),
            dma((n_row - 1,)),
        ],
        compiler_params=pltpu.CompilerParams(collective_id=0, has_side_effects=True),
    )(x_slab, cell_factor, index, scale, gene_factor)


def local(x_slab, cell_factor, row_index, gene_scale, gene_factor, first_moment, second_moment):
    rows_dev, genes_dev = x_slab.shape
    n_gene = lax.axis_size("gene")
    n_row = lax.axis_size("row")
    scale_k = 4.0 / math.sqrt(genes_dev * n_gene)
    grad_rows, grad_cols = fused(
        n_gene,
        n_row,
        x_slab,
        cell_factor,
        row_index.reshape(rows_dev // LANES, LANES),
        gene_scale.reshape(1, genes_dev),
        gene_factor,
    )
    grad_cells = -scale_k * grad_rows
    grad_genes = -scale_k * grad_cols
    new_first = beta_one * first_moment + (1.0 - beta_one) * grad_genes
    new_second = beta_two * second_moment + (1.0 - beta_two) * grad_genes * grad_genes
    first_hat = new_first / (1.0 - beta_one**10)
    second_hat = new_second / (1.0 - beta_two**10)
    new_factor = gene_factor - learn_rate * first_hat / (jnp.sqrt(second_hat) + adam_eps)
    return (grad_cells, new_factor, new_first, new_second)


def solution(mesh):
    in_specs = (
        P(("grp", "row"), "gene"),
        P(("grp", "row"), None),
        P(("grp", "row")),
        P(("grp", "gene")),
        P(("grp", "gene", "row"), None),
        P(("grp", "gene", "row"), None),
        P(("grp", "gene", "row"), None),
    )
    out_specs = (
        P(("grp", "row", "gene"), None),
        P(("grp", "gene", "row"), None),
        P(("grp", "gene", "row"), None),
        P(("grp", "gene", "row"), None),
    )
    return jax.shard_map(local, mesh=mesh, in_specs=in_specs, out_specs=out_specs, check_vma=False)
```

time: 103 us -> 33.6 us (0.33)
  the two profiles are of different devices: /device:TPU:0 before, /device:TPU:11 now
where the time goes in v1:
time: 33.6 us; the launch traced here: 33.3 us
  Pallas kernels  28 us (83%)
  other arithmetic  3.38 us (10%)
  local copies, waits for them, and re-layouts  1.32 us (4%)
  between operations  0.67 us (2%)
    pallas_call x1, Pallas kernels, fused(): pl.pallas_call(functools.partial(kernel, n_gene, n_row), out_shape=(jax.S...  28 us
    mul x1, other arithmetic, local(): grad_cells = -scale_k * grad_rows  1.78 us
    sub x1, other arithmetic, local(): gene_factor - learn_rate * first_hat / (jnp.sqrt(second_hat) + adam_eps)  1.6 us
    reshape x1, local copies, waits for them, and re-layouts, local(): gene_scale.reshape(1, genes_dev)  1.31 us

profile of v1, /device:TPU:11, one launch (start us, length us, event | category | flops | bytes accessed | tf_op | source)
XLA Modules:
  0.0 33.3 jit_solution(15188265378504317924)
XLA Ops:
  0.6 0.0 copy-start
  0.6 0.0 copy-start.2
  0.7 0.0 copy-start.1
  0.7 1.3 %reshape.15.scale_ref = f32[1,640]{1,0:T(1,128)} reshape(f32[640]{0:T(1024)} %param.10) | data formatting | bytes 5120 | tf_op jit(solution)/shard_map/reshape | solution.py:289
  2.0 28.0 %shard_map.102 = (f32[768,128]{1,0:T(8,128)}, f32[160,128]{1,0:T(8,128)}) custom-call(bf16[3072,640]{1,0:T(8,128)(2,1)} %x_hbm.1, bf16[512,128]{1,0:T(8,128)(2,1)} %cell_ref.1, s32[24,128]{1,0:T(8,128)} %bitcast.1, f32[1,640]{1,0:T(1,128)} %reshape.15.scale_ref, f32[160,128]{1,0:T(8,128)} %gene_ref.1), custom_call_target="tpu_custom_call" | custom-call | tf_op jit(solution)/shard_map/pallas_call | solution.py:246
  29.9 1.8 %broadcast_multiply_fusion = f32[768,128]{1,0:T(8,128)} fusion(f32[768,128]{1,0:T(8,128)} %get-tuple-element.6), kind=kLoop, calls=%fused_computation | loop fusion | flops 98304 | bytes 786432 | tf_op jit(solution)/shard_map/mul | solution.py:292
  31.7 0.0 copy-done
  31.7 0.0 copy-done.2
  31.7 0.0 copy-done.1
  31.7 1.6 %divide_subtract_fusion = (f32[160,128]{1,0:T(8,128)}, f32[160,128]{1,0:T(8,128)}, f32[160,128]{1,0:T(8,128)}) fusion(f32[160,128]{1,0:T(8,128)S(1)} %copy-done, f32[160,128]{1,0:T(8,128)} %get-tuple-element.7, f32[160,128]{1,0:T(8,128)S(1)} %copy-done.1, f32[160,128]{1,0:T(8,128)S(1)} %copy-done.2), kind=kLoop, calls=%fused_computation.1 | loop fusion | flops 266240 | bytes 573440 | tf_op jit(solution)/shard_map/sub | solution.py:298
Async XLA Ops:
  0.6 31.1 %copy-start = (f32[160,128]{1,0:T(8,128)S(1)}, f32[160,128]{1,0:T(8,128)}, u32[]{:S(2)}) copy-start(f32[160,128]{1,0:T(8,128)} %gene_ref.1) | copy-start | bytes 245764
  0.6 31.1 %copy-start.2 = (f32[160,128]{1,0:T(8,128)S(1)}, f32[160,128]{1,0:T(8,128)}, u32[]{:S(2)}) copy-start(f32[160,128]{1,0:T(8,128)} %param.13) | copy-start | bytes 245764
  0.7 31.1 %copy-start.1 = (f32[160,128]{1,0:T(8,128)S(1)}, f32[160,128]{1,0:T(8,128)}, u32[]{:S(2)}) copy-start(f32[160,128]{1,0:T(8,128)} %param.12) | copy-start | bytes 245764

commit v2 on v1

--- a/solution.py
+++ b/solution.py
@@ -30,12 +30,22 @@
     n_gene,
     n_row,
     x_hbm,
+    cell_hbm,
+    index_hbm,
+    scale_hbm,
+    gene_hbm,
+    first_hbm,
+    second_hbm,
+    rows_out,
+    factor_out,
+    first_out,
+    second_out,
     cell_ref,
     index_ref,
     scale_ref,
     gene_ref,
-    rows_out,
-    genes_out,
+    first_ref,
+    second_ref,
     x_buf,
     fac,
     fac_t,
@@ -47,6 +57,7 @@
     own,
     col_send,
     col_recv,
+    load_sem,
     x_sem,
     ag_send_sem,
     ag_recv_sem,
@@ -58,6 +69,7 @@
     rows, genes = x_buf.shape
     cells, rank = cell_ref.shape
     genes_own = gene_ref.shape[0]
+    scale_k = 4.0 / math.sqrt(genes * n_gene)
     per, chunk, pieces, group = plan(rows, n_gene)
     n_chunk = rows // chunk
     own_chunks = pieces
@@ -82,12 +94,32 @@
         window = pl.ds(pl.multiple_of(chunk_at(i) * chunk, chunk), chunk)
         return pltpu.make_async_copy(x_hbm.at[window], x_buf.at[pl.ds(i * chunk, chunk)], x_sem.at[i])
 
+    loads = [
+        pltpu.make_async_copy(src, dst, load_sem.at[k])
+        for k, (src, dst) in enumerate(
+            (
+                (gene_hbm, gene_ref),
+                (cell_hbm, cell_ref),
+                (index_hbm, index_ref),
+                (scale_hbm, scale_ref),
+                (first_hbm, first_ref),
+                (second_hbm, second_ref),
+            )
+        )
+    ]
+    for load in loads[:4]:
+        load.start()
     for i in range(n_chunk):
         x_copy(i).start()
-
+    for load in loads[4:]:
+        load.start()
+
+    loads[0].wait()
     own_genes = pl.ds(pl.multiple_of(me_row * genes_own, genes_own), genes_own)
     gath[own_genes] = gene_ref[...].astype(jnp.bfloat16)
 
+    loads[1].wait()
+    loads[2].wait()
     cell_t = cell_ref[...].astype(jnp.float32).T.astype(jnp.bfloat16)
     cell_id = lax.broadcasted_iota(jnp.int32, (cells, LANES), 0) + me_row * cells
 
@@ -122,7 +154,9 @@
         ag_copy(step).start()
     for c in range(half, n_chunk):
         gather_factors(c)
-    inv = 1.0 / scale_ref[...]
+    loads[3].wait()
+    scale = jnp.concatenate([scale_ref[k : k + 1, :] for k in range(genes // LANES)], axis=1)
+    inv = 1.0 / scale
     inv_tc = inv * (1.0 / tukey_c)
     inv_sq = inv * inv
     for step in range(1, n_row):
@@ -198,7 +232,16 @@
     for step in range(1, n_row):
         col_copy(step).wait()
         cols_own = cols_own + col_recv[step - 1].astype(jnp.float32)
-    genes_out[...] = cols_own
+    loads[4].wait()
+    loads[5].wait()
+    grad_genes = -scale_k * cols_own
+    new_first = beta_one * first_ref[...] + (1.0 - beta_one) * grad_genes
+    new_second = beta_two * second_ref[...] + (1.0 - beta_two) * grad_genes * grad_genes
+    first_hat = new_first / (1.0 - beta_one**10)
+    second_hat = new_second / (1.0 - beta_two**10)
+    first_out[...] = new_first
+    second_out[...] = new_second
+    factor_out[...] = gene_ref[...] - learn_rate * first_hat / (jnp.sqrt(second_hat) + adam_eps)
 
     size = chunk if group == 1 else per
 
@@ -219,7 +262,7 @@
         acc = own[piece]
         for step in range(1, n_gene):
             acc = acc + arrived(step, piece)
-        rows_out[piece * size : (piece + 1) * size] = acc
+        rows_out[piece * size : (piece + 1) * size] = -scale_k * acc
 
     for i in range(n_chunk):
         if group == 1:
@@ -233,7 +276,7 @@
                     block_copy(i, j).wait_send()
 
 
-def fused(n_gene, n_row, x_slab, cell_factor, index, scale, gene_factor):
+def fused(n_gene, n_row, x_slab, cell_factor, index, scale, gene_factor, first, second):
     rows, genes = x_slab.shape
     cells, rank = cell_factor.shape
     genes_own = gene_factor.shape[0]
@@ -245,13 +288,16 @@
     dma = pltpu.SemaphoreType.DMA
     return pl.pallas_call(
         functools.partial(kernel, n_gene, n_row),
-        out_shape=(
-            jax.ShapeDtypeStruct((per, rank), jnp.float32),
-            jax.ShapeDtypeStruct((genes_own, rank), jnp.float32),
-        ),
-        in_specs=[pl.BlockSpec(memory_space=pl.ANY), vmem, vmem, vmem, vmem],
-        out_specs=(vmem, vmem),
+        out_shape=(pltpu.VMEM((per, rank), jnp.float32),) + (pltpu.VMEM((genes_own, rank), jnp.float32),) * 3,
+        in_specs=[pl.BlockSpec(memory_space=pl.ANY)] * 7,
+        out_specs=(vmem,) * 4,
         scratch_shapes=[
+            pltpu.VMEM(cell_factor.shape, bf),
+            pltpu.VMEM(index.shape, jnp.int32),
+            pltpu.VMEM(scale.shape, jnp.float32),
+            pltpu.VMEM(gene_factor.shape, jnp.float32),
+            pltpu.VMEM(gene_factor.shape, jnp.float32),
+            pltpu.VMEM(gene_factor.shape, jnp.float32),
             pltpu.VMEM((rows, genes), bf),
             pltpu.VMEM((n_chunk, chunk, rank), bf),
             pltpu.VMEM((n_chunk, rank, chunk), bf),
@@ -263,6 +309,7 @@
             pltpu.VMEM((pieces, size, rank), jnp.float32),
             pltpu.VMEM((genes, rank), bf),
             pltpu.VMEM((n_row - 1, genes_own, rank), bf),
+            dma((6,)),
             dma((n_chunk,)),
             dma((n_row - 1,)),
             dma((n_row - 1,)),
@@ -272,31 +319,45 @@
             dma((n_row - 1,)),
         ],
         compiler_params=pltpu.CompilerParams(collective_id=0, has_side_effects=True),
-    )(x_slab, cell_factor, index, scale, gene_factor)
+    )(x_slab, cell_factor, index, scale, gene_factor, first, second)
+
+
+def write_kernel(*refs):
+    count = (len(refs) - 1) // 2
+    sem = refs[-1]
+    copies = [pltpu.make_async_copy(refs[k], refs[count + k], sem.at[k]) for k in range(count)]
+    for copy in copies:
+        copy.start()
+    for copy in copies:
+        copy.wait()
+
+
+def write_out(held):
+    return pl.pallas_call(
+        write_kernel,
+        out_shape=tuple(jax.ShapeDtypeStruct(h.shape, h.dtype) for h in held),
+        in_specs=[pl.BlockSpec(memory_space=pltpu.VMEM)] * len(held),
+        out_specs=(pl.BlockSpec(memory_space=pl.ANY),) * len(held),
+        scratch_shapes=[pltpu.SemaphoreType.DMA((len(held),))],
+    )(*[pltpu.with_memory_space_constraint(h, pltpu.VMEM) for h in held])
 
 
 def local(x_slab, cell_factor, row_index, gene_scale, gene_factor, first_moment, second_moment):
     rows_dev, genes_dev = x_slab.shape
     n_gene = lax.axis_size("gene")
     n_row = lax.axis_size("row")
-    scale_k = 4.0 / math.sqrt(genes_dev * n_gene)
-    grad_rows, grad_cols = fused(
+    held = fused(
         n_gene,
         n_row,
         x_slab,
         cell_factor,
         row_index.reshape(rows_dev // LANES, LANES),
-        gene_scale.reshape(1, genes_dev),
+        gene_scale.reshape(genes_dev // LANES, LANES),
         gene_factor,
+        first_moment,
+        second_moment,
     )
-    grad_cells = -scale_k * grad_rows
-    grad_genes = -scale_k * grad_cols
-    new_first = beta_one * first_moment + (1.0 - beta_one) * grad_genes
-    new_second = beta_two * second_moment + (1.0 - beta_two) * grad_genes * grad_genes
-    first_hat = new_first / (1.0 - beta_one**10)
-    second_hat = new_second / (1.0 - beta_two**10)
-    new_factor = gene_factor - learn_rate * first_hat / (jnp.sqrt(second_hat) + adam_eps)
-    return (grad_cells, new_factor, new_first, new_second)
+    return write_out(held)
 
 
 def solution(mesh):

time: 33.6 us -> 29.5 us (0.88)
  the two profiles are of different devices: /device:TPU:11 before, /device:TPU:9 now
where the time goes in v2:
time: 29.5 us; the launch traced here: 29.4 us
  Pallas kernels  28.7 us (97%)
  between operations  0.64 us (2%)
    pallas_call x1, Pallas kernels, fused(): pl.pallas_call(functools.partial(kernel, n_gene, n_row), out_shape=(pltpu...  27.9 us
    pallas_call x1, Pallas kernels, write_out(): pl.pallas_call(write_kernel, out_shape=tuple((jax.ShapeDtypeStruct(h.shap...  0.86 us

profile of v2, /device:TPU:9, one launch (start us, length us, event | category | flops | bytes accessed | tf_op | source)
XLA Modules:
  0.0 29.4 jit_solution(9741396875456416305)
XLA Ops:
  0.6 27.9 %shard_map.102 = (f32[768,128]{1,0:T(8,128)S(1)}, f32[160,128]{1,0:T(8,128)S(1)}, f32[160,128]{1,0:T(8,128)S(1)}, f32[160,128]{1,0:T(8,128)S(1)}) custom-call(bf16[3072,640]{1,0:T(8,128)(2,1)} %x_hbm.1, bf16[512,128]{1,0:T(8,128)(2,1)} %cell_hbm.1, s32[24,128]{1,0:T(8,128)} %bitcast.2, f32[5,128]{1,0:T(8,128)} %bitcast.3, f32[160,128]{1,0:T(8,128)} %gene_hbm.1, ...), custom_call_target="tpu_custom_call" | custom-call | tf_op jit(solution)/shard_map/pallas_call | solution.py:289
  28.5 0.9 %shard_map.103 = (f32[768,128]{1,0:T(8,128)}, f32[160,128]{1,0:T(8,128)}, f32[160,128]{1,0:T(8,128)}, f32[160,128]{1,0:T(8,128)}) custom-call(f32[768,128]{1,0:T(8,128)S(1)} %get-tuple-element.8.refs_0_, f32[160,128]{1,0:T(8,128)S(1)} %get-tuple-element.9.refs_1_, f32[160,128]{1,0:T(8,128)S(1)} %get-tuple-element.10.refs_2_, ...), custom_call_target="tpu_custom_call" | custom-call | tf_op jit(solution)/shard_map/pallas_call | solution.py:336

commit v3 on v2

--- a/solution.py
+++ b/solution.py
@@ -79,8 +79,30 @@
     barrier = pltpu.get_barrier_semaphore()
     for step in range(1, n_row):
         pl.semaphore_signal(barrier, inc=1, device_id={"row": lax.rem(me_row + step, n_row)}, device_id_type=MESH)
-    for step in range(1, n_gene):
-        pl.semaphore_signal(barrier, inc=1, device_id={"gene": lax.rem(me_gene + step, n_gene)}, device_id_type=MESH)
+    relay = n_gene == 4 and group == 1
+    if relay:
+        high, low = me_gene // 2, lax.rem(me_gene, 2)
+        inner = high + low - 2 * high * low
+        outer = 1 - inner
+
+        def partner(mask):
+            flipped_high = 1 - high if mask >= 2 else high
+            flipped_low = 1 - low if mask % 2 == 1 else low
+            return 2 * flipped_high + flipped_low
+
+        for mask in (1, 2):
+            pl.semaphore_signal(barrier, inc=1, device_id={"gene": partner(mask)}, device_id_type=MESH)
+
+        @pl.when(inner == 1)
+        def _():
+            pl.semaphore_signal(barrier, inc=1, device_id={"gene": partner(3)}, device_id_type=MESH)
+
+        arrivals = n_row - 1 + 2 + inner
+    else:
+        for step in range(1, n_gene):
+            peer = lax.rem(me_gene + step, n_gene)
+            pl.semaphore_signal(barrier, inc=1, device_id={"gene": peer}, device_id_type=MESH)
+        arrivals = n_row - 1 + n_gene - 1
 
     if group == 1:
         first = me_gene * pieces + pieces
@@ -88,6 +110,8 @@
         first = me_gene // group + 1
 
     def chunk_at(i):
+        if relay:
+            return partner(3 - i // pieces) * pieces + i % pieces
         return lax.rem(first + i, n_chunk)
 
     def x_copy(i):
@@ -137,7 +161,7 @@
     for c in range(half):
         gather_factors(c)
 
-    pl.semaphore_wait(barrier, n_row + n_gene - 2)
+    pl.semaphore_wait(barrier, arrivals)
 
     def ag_copy(step):
         peer = lax.rem(me_row + step, n_row)
@@ -165,6 +189,19 @@
     gath_t[...] = factor.astype(jnp.float32).T.astype(jnp.bfloat16)
 
     def block_copy(i, j):
+        if relay:
+            turn, piece = i // pieces, i % pieces
+            target, slot = partner(3 - turn), turn
+            if turn == 0:
+                target, slot = outer * partner(1) + inner * target, 3 * outer
+            return pltpu.make_async_remote_copy(
+                src_ref=send_buf.at[i],
+                dst_ref=recv_buf.at[slot, piece],
+                send_sem=send_sem.at[i, 0],
+                recv_sem=recv_sem.at[slot, piece],
+                device_id={"gene": target},
+                device_id_type=MESH,
+            )
         c = chunk_at(i)
         owner = c // pieces if group == 1 else c * group + j
         piece = lax.rem(c, pieces) if group == 1 else 0
@@ -178,6 +215,17 @@
             device_id_type=MESH,
         )
 
+    def landed(slot, piece):
+        pltpu.make_async_remote_copy(
+            src_ref=recv_buf.at[slot, piece],
+            dst_ref=recv_buf.at[slot, piece],
+            send_sem=send_sem.at[0, 0],
+            recv_sem=recv_sem.at[slot, piece],
+            device_id={"gene": lax.rem(me_gene + 1, n_gene)},
+            device_id_type=MESH,
+        ).wait_recv()
+        return recv_buf[slot, piece].astype(jnp.float32)
+
     for i in range(n_chunk):
         c = chunk_at(i)
         x_copy(i).wait()
@@ -190,6 +238,16 @@
         part = jnp.dot(infl, gath[...], preferred_element_type=jnp.float32)
         if group == 1 and i >= n_chunk - own_chunks:
             own[i - (n_chunk - own_chunks)] = part
+        elif relay and i // pieces == 1:
+
+            @pl.when(inner == 1)
+            def _():
+                send_buf[i] = (part + landed(3, i % pieces)).astype(jnp.bfloat16)
+
+            @pl.when(inner == 0)
+            def _():
+                send_buf[i] = part.astype(jnp.bfloat16)
+
         else:
             send_buf[i] = part.astype(jnp.bfloat16)
             if group > 1:
@@ -245,24 +303,20 @@
 
     size = chunk if group == 1 else per
 
-    def arrived(step, piece):
-        sender = lax.rem(me_gene + n_gene - step, n_gene)
-        copy = pltpu.make_async_remote_copy(
-            src_ref=recv_buf.at[sender, piece],
-            dst_ref=recv_buf.at[sender, piece],
-            send_sem=send_sem.at[0, 0],
-            recv_sem=recv_sem.at[sender, piece],
-            device_id={"gene": sender},
-            device_id_type=MESH,
-        )
-        copy.wait_recv()
-        return recv_buf[sender, piece].astype(jnp.float32)
-
     for piece in range(pieces):
+        window = pl.ds(piece * size, size)
         acc = own[piece]
-        for step in range(1, n_gene):
-            acc = acc + arrived(step, piece)
-        rows_out[piece * size : (piece + 1) * size] = -scale_k * acc
+        if relay:
+            acc = acc + landed(1, piece) + landed(2, piece)
+            rows_out[window] = -scale_k * acc
+
+            @pl.when(inner == 1)
+            def _():
+                rows_out[window] = -scale_k * (acc + landed(0, piece))
+        else:
+            for step in range(1, n_gene):
+                acc = acc + landed(lax.rem(me_gene + n_gene - step, n_gene), piece)
+            rows_out[window] = -scale_k * acc
 
     for i in range(n_chunk):
         if group == 1:

time: 29.5 us -> 26.8 us (0.908)
  the two profiles are of different devices: /device:TPU:9 before, /device:TPU:0 now
where the time goes in v3:
time: 26.8 us; the launch traced here: 26.6 us
  Pallas kernels  26 us (97%)
  between operations  0.64 us (2%)
    pallas_call x1, Pallas kernels, fused(): pl.pallas_call(functools.partial(kernel, n_gene, n_row), out_shape=(pltpu...  25.1 us
    pallas_call x1, Pallas kernels, write_out(): pl.pallas_call(write_kernel, out_shape=tuple((jax.ShapeDtypeStruct(h.shap...  0.86 us

profile of v3, /device:TPU:0, one launch (start us, length us, event | category | flops | bytes accessed | tf_op | source)
XLA Modules:
  0.0 26.6 jit_solution(1895154825247565203)
XLA Ops:
  0.6 25.1 %shard_map.102 = (f32[768,128]{1,0:T(8,128)S(1)}, f32[160,128]{1,0:T(8,128)S(1)}, f32[160,128]{1,0:T(8,128)S(1)}, f32[160,128]{1,0:T(8,128)S(1)}) custom-call(bf16[3072,640]{1,0:T(8,128)(2,1)} %x_hbm.1, bf16[512,128]{1,0:T(8,128)(2,1)} %cell_hbm.1, s32[24,128]{1,0:T(8,128)} %bitcast.2, f32[5,128]{1,0:T(8,128)} %bitcast.3, f32[160,128]{1,0:T(8,128)} %gene_hbm.1, ...), custom_call_target="tpu_custom_call" | custom-call | tf_op jit(solution)/shard_map/pallas_call | solution.py:343
  25.8 0.9 %shard_map.103 = (f32[768,128]{1,0:T(8,128)}, f32[160,128]{1,0:T(8,128)}, f32[160,128]{1,0:T(8,128)}, f32[160,128]{1,0:T(8,128)}) custom-call(f32[768,128]{1,0:T(8,128)S(1)} %get-tuple-element.8.refs_0_, f32[160,128]{1,0:T(8,128)S(1)} %get-tuple-element.9.refs_1_, f32[160,128]{1,0:T(8,128)S(1)} %get-tuple-element.10.refs_2_, ...), custom_call_target="tpu_custom_call" | custom-call | tf_op jit(solution)/shard_map/pallas_call | solution.py:390

commit v4 on v3

--- a/solution.py
+++ b/solution.py
@@ -157,10 +157,6 @@
         fac_t[c] = both.astype(jnp.bfloat16)
         fac[c] = both.T.astype(jnp.bfloat16)
 
-    half = n_chunk // 2
-    for c in range(half):
-        gather_factors(c)
-
     pl.semaphore_wait(barrier, arrivals)
 
     def ag_copy(step):
@@ -176,7 +172,7 @@
 
     for step in range(1, n_row):
         ag_copy(step).start()
-    for c in range(half, n_chunk):
+    for c in range(n_chunk):
         gather_factors(c)
     loads[3].wait()
     scale = jnp.concatenate([scale_ref[k : k + 1, :] for k in range(genes // LANES)], axis=1)

time: 26.8 us -> 26.4 us (0.985)
  Pallas kernels: 26 us -> 25.6 us
    pallas_call x1, Pallas kernels: 25.1 us -> 24.8 us  [fused(): pl.pallas_call(functools.partial(kernel, n_gene, n_row), out_shape=(pltpu...]
where the time goes in v4:
time: 26.4 us; the launch traced here: 26.3 us
  Pallas kernels  25.6 us (97%)
  between operations  0.64 us (2%)
    pallas_call x1, Pallas kernels, fused(): pl.pallas_call(functools.partial(kernel, n_gene, n_row), out_shape=(pltpu...  24.8 us
    pallas_call x1, Pallas kernels, write_out(): pl.pallas_call(write_kernel, out_shape=tuple((jax.ShapeDtypeStruct(h.shap...  0.86 us

profile of v4, /device:TPU:0, one launch (start us, length us, event | category | flops | bytes accessed | tf_op | source)
XLA Modules:
  0.0 26.3 jit_solution(13138376416562479162)
XLA Ops:
  0.6 24.8 %shard_map.102 = (f32[768,128]{1,0:T(8,128)S(1)}, f32[160,128]{1,0:T(8,128)S(1)}, f32[160,128]{1,0:T(8,128)S(1)}, f32[160,128]{1,0:T(8,128)S(1)}) custom-call(bf16[3072,640]{1,0:T(8,128)(2,1)} %x_hbm.1, bf16[512,128]{1,0:T(8,128)(2,1)} %cell_hbm.1, s32[24,128]{1,0:T(8,128)} %bitcast.2, f32[5,128]{1,0:T(8,128)} %bitcast.3, f32[160,128]{1,0:T(8,128)} %gene_hbm.1, ...), custom_call_target="tpu_custom_call" | custom-call | tf_op jit(solution)/shard_map/pallas_call | solution.py:339
  25.4 0.9 %shard_map.103 = (f32[768,128]{1,0:T(8,128)}, f32[160,128]{1,0:T(8,128)}, f32[160,128]{1,0:T(8,128)}, f32[160,128]{1,0:T(8,128)}) custom-call(f32[768,128]{1,0:T(8,128)S(1)} %get-tuple-element.8.refs_0_, f32[160,128]{1,0:T(8,128)S(1)} %get-tuple-element.9.refs_1_, f32[160,128]{1,0:T(8,128)S(1)} %get-tuple-element.10.refs_2_, ...), custom_call_target="tpu_custom_call" | custom-call | tf_op jit(solution)/shard_map/pallas_call | solution.py:386
